TPU v7x, 32 devices: a whole 2x2x4 slice. The times are simulated.
32 devices in a mesh: rollout: 2 (over y), branch: 4 (over z), seq: 4 (over x, core).
Axes of the slice: x: 2, y: 2, z: 4, core: 2. Of those that a mesh axis runs over, the one named last changes fastest.
Arguments:
- queries: bfloat16 [8, 512, 4096], P(('rollout', 'branch'), 'seq'), parts along dimension 0, may hold values from -8 to 8
- keyvals: bfloat16 [8, 512, 2, 256], P(('rollout', 'branch'), 'seq'), parts along dimension 0, may hold values from -4 to 4
- residual: bfloat16 [8, 512, 4096], P(('rollout', 'branch'), 'seq'), parts along dimension 0, may hold values from -3 to 3
- read_list: int32 [8, 4, 3], P(('rollout', 'branch'), 'seq'), parts along dimension 0, may hold values from 0 to 3
- router: bfloat16 [4096, 8], replicated, may hold values from -0.09375 to 0.09375
- expert_ids: int32 [8, 512, 2], P(('rollout', 'branch'), 'seq'), parts along dimension 0, may hold values from 0 to 7, all different within a row; in each aligned block of 128 rows (0 to 127, 128 to 255, ..., all dimensions but the last counted through in order) at most 48 rows name the same one
- w_gate_up: bfloat16 [16, 4096, 2, 384], P(('branch', 'seq')), may hold values from -0.09375 to 0.09375
- w_down: bfloat16 [16, 384, 4096], P(('branch', 'seq')), may hold values from -0.21875 to 0.21875
Outputs:
- mixed: bfloat16 [8, 512, 4096], P(('rollout', 'branch'), 'seq'), parts along dimension 0
There are 2 independent parts, one for each index of `rollout`. A program takes and returns all parts, laid end to end along the dimension named above; an argument that names none is the same for every part. Nothing has to cross between parts.
Inputs may be any that keep to these rules, and one draw needn't show every extreme that they name: read_list[c, s, o] is the block of branch c that query block s of branch (c + o + 1) mod 4 reads. `expert_ids`: each token names 2 different experts; of the 128 tokens of one device at most 48 name one expert, and in every draw some expert is named by exactly 48 tokens of some device.
All inputs are finite; a program needn't handle non-finite values.
Results may differ from a plain program's by a relative error of at most 0.0062.
Values may be sent and summed in bfloat16 or wider, within the bound.
A program may use at most 192 MiB of HBM per device.

v0:
```python
import math
import jax
import jax.numpy as jnp
from jax import lax
from jax.sharding import PartitionSpec as P

D = 4096
HEAD_SIZE = 128
QUERY_HEADS = 32
KEY_VALUE_HEADS = 2


def swapped(value, axis, apart):
    mask = 2**apart
    pairs = [(source, source ^ mask) for source in range(lax.axis_size(axis))]
    return lax.ppermute(value, axis, pairs)


def attend_block(q_rows, own_kv, sib_kv, block_index):
    block_len = q_rows.shape[0]
    length_own = own_kv.shape[0]
    positions = block_index * block_len + jnp.arange(block_len, dtype=jnp.int32)
    own_allowed = jnp.arange(length_own, dtype=jnp.int32)[None, :] <= positions[:, None]
    allowed = jnp.concatenate(
        [own_allowed, jnp.ones((block_len, sib_kv.shape[0]), dtype=bool)], axis=1
    )
    key_rows = jnp.concatenate([own_kv[:, 0], sib_kv[:, 0]], axis=0)
    value_rows = jnp.concatenate([own_kv[:, 1], sib_kv[:, 1]], axis=0)
    group_count = QUERY_HEADS // KEY_VALUE_HEADS
    sub_heads = min(group_count, 8)
    inv_scale = 1.0 / math.sqrt(HEAD_SIZE)
    pieces = []
    for head_key_value in range(KEY_VALUE_HEADS):
        key_head = key_rows[:, head_key_value * HEAD_SIZE : (head_key_value + 1) * HEAD_SIZE]
        value_head = value_rows[:, head_key_value * HEAD_SIZE : (head_key_value + 1) * HEAD_SIZE]
        for start_head in range(0, group_count, sub_heads):
            column = (head_key_value * group_count + start_head) * HEAD_SIZE
            query_head = q_rows[:, column : column + sub_heads * HEAD_SIZE].reshape(
                block_len, sub_heads, HEAD_SIZE
            )
            raw_scores = jnp.einsum(
                "tgd,kd->gtk", query_head, key_head, preferred_element_type=jnp.float32
            )
            masked = jnp.where(allowed[None], raw_scores, -1e30)
            row_max = jnp.max(masked, axis=-1, keepdims=True) * inv_scale
            expterm = jnp.exp(masked * inv_scale - row_max)
            probs = (expterm / jnp.sum(expterm, axis=-1, keepdims=True)).astype(jnp.bfloat16)
            mixture = jnp.einsum(
                "gtk,kd->tgd", probs, value_head, preferred_element_type=jnp.float32
            )
            pieces.append(mixture.reshape(block_len, sub_heads * HEAD_SIZE).astype(jnp.bfloat16))
    return jnp.concatenate(pieces, axis=1)


def on_device(queries, keyvals, residual, read_list, router, expert_ids, w_gate_up, w_down):
    block_len = queries.shape[1]
    kv_width = keyvals.shape[-1]
    seq_blocks = lax.axis_size("seq")
    branches = lax.axis_size("branch")
    me_branch = lax.axis_index("branch")
    me_block = lax.axis_index("seq")
    suffix_all = lax.all_gather(keyvals, "seq", axis=1, tiled=True)[0]
    blocks = suffix_all.reshape(seq_blocks, block_len, 2, kv_width)
    picked = blocks[read_list[0, 0]]
    by_offset = jnp.concatenate(
        [jnp.zeros((1, block_len, 2, kv_width), keyvals.dtype), picked], axis=0
    )
    by_dest = (jnp.arange(branches, dtype=jnp.int32) - me_branch) % branches
    outgoing = by_offset[by_dest]
    incoming = lax.all_to_all(outgoing, "branch", split_axis=0, concat_axis=0, tiled=True)
    others = (me_branch + 1 + jnp.arange(branches - 1, dtype=jnp.int32)) % branches
    sibling = incoming[others].reshape((branches - 1) * block_len, 2, kv_width)
    context = attend_block(queries[0], suffix_all, sibling, me_block)
    state = residual[0].astype(jnp.float32) + context.astype(jnp.float32)
    normed = (state * lax.rsqrt(jnp.mean(state * state, axis=-1, keepdims=True) + 1e-06)).astype(
        jnp.bfloat16
    )
    logits = jnp.dot(normed, router, preferred_element_type=jnp.float32)
    routed = expert_ids[0]
    top_count = routed.shape[1]
    experts = router.shape[1]
    chosen_logits = jnp.take_along_axis(logits, routed, axis=1)
    gate_mix = 1.0 / jnp.sum(
        jnp.exp(chosen_logits[:, None, :] - chosen_logits[:, :, None]), axis=-1
    )
    capacity = 2 * ((3 * block_len * top_count + 4 * experts - 1) // (4 * experts))
    half_cap = capacity // 2
    flat_ids = routed.reshape(-1)
    onehot = (flat_ids[:, None] == jnp.arange(experts, dtype=jnp.int32)[None, :]).astype(jnp.int32)
    slot_of = jnp.sum((jnp.cumsum(onehot, axis=0) - 1) * onehot, axis=1)
    row_token = jnp.arange(block_len * top_count, dtype=jnp.int32) // top_count
    sendbuf = (
        jnp.zeros((experts, capacity, D), jnp.bfloat16).at[flat_ids, slot_of].set(normed[row_token])
    )
    pair_half = me_block % 2
    halved = sendbuf.reshape(experts * 2, half_cap, D)
    own_share = lax.all_to_all(halved, ("branch", "seq"), split_axis=0, concat_axis=0, tiled=True)
    theirs = swapped(own_share, "seq", 0)
    rows_in = jnp.where(
        pair_half == 0,
        jnp.concatenate([own_share, theirs], axis=1),
        jnp.concatenate([theirs, own_share], axis=1),
    )
    devices = rows_in.shape[0]
    half_width = D // 2
    expert_rows = rows_in.reshape(devices * capacity, D)
    gate_up = jnp.einsum(
        "rd,dcf->rcf", expert_rows, w_gate_up[0], preferred_element_type=jnp.float32
    )
    hidden_act = (jax.nn.silu(gate_up[:, 0]) * gate_up[:, 1]).astype(jnp.bfloat16)
    down_local = w_down[0]
    kept_cols = lax.dynamic_slice_in_dim(down_local, pair_half * half_width, half_width, 1)
    given_cols = lax.dynamic_slice_in_dim(down_local, (1 - pair_half) * half_width, half_width, 1)
    kept_share = jnp.dot(hidden_act, kept_cols, preferred_element_type=jnp.float32).reshape(
        devices, capacity, half_width
    )
    given_share = jnp.dot(hidden_act, given_cols, preferred_element_type=jnp.float32).reshape(
        devices, capacity, half_width
    )
    gotten = swapped(given_share, "seq", 0)
    finished = (kept_share + gotten).astype(jnp.bfloat16)
    returned = lax.all_to_all(finished, ("branch", "seq"), split_axis=0, concat_axis=0, tiled=True)
    out_table = jnp.swapaxes(returned.reshape(experts, 2, capacity, half_width), 1, 2).reshape(
        experts, capacity, D
    )
    expert_out = out_table[flat_ids, slot_of].reshape(block_len, top_count, D)
    layer_out = state
    for slot_k in range(top_count):
        layer_out = layer_out + gate_mix[:, slot_k : slot_k + 1] * expert_out[:, slot_k].astype(
            jnp.float32
        )
    return layer_out.astype(jnp.bfloat16)[None]


def solution(mesh):
    return jax.shard_map(
        on_device,
        mesh=mesh,
        in_specs=(
            P(("rollout", "branch"), "seq", None),
            P(("rollout", "branch"), "seq", None, None),
            P(("rollout", "branch"), "seq", None),
            P(("rollout", "branch"), "seq", None),
            P(),
            P(("rollout", "branch"), "seq", None),
            P(("branch", "seq"), None, None, None),
            P(("branch", "seq"), None, None),
        ),
        out_specs=P(("rollout", "branch"), "seq", None),
        check_vma=False,
    )
```

profile of v0, /device:TPU:11, one launch (start us, length us, event | category | flops | bytes accessed | tf_op | source)
XLA Modules:
  0.0 366.1 jit_solution(11561085254637891067)
XLA Ops:
  1.1 7.7 %all_gather.3 = bf16[1,512,2,256]{3,1,2,0:T(8,128)(2,1)} all-gather(bf16[1,128,2,256]{3,1,2,0:T(8,128)(2,1)S(1)} %copy.62), channel_id=1, replica_groups=mesh['rollout'=2,'branch'=4,'seq'=4] {'seq'}, dimensions={1}, use_global_device_ids=true | all-gather | bytes 655360 | tf_op jit(solution)/shard_map/all_gather | solution.py:62
  14.4 4.8 %all-to-all-start = ((bf16[4,128,2,256]{3,1,2,0:T(8,128)(2,1)}), bf16[4,128,2,256]{3,1,2,0:T(8,128)(2,1)}, u32[]{:S(2)}, u32[]{:S(2)}) async-start(bf16[4,128,2,256]{3,1,2,0:T(8,128)(2,1)} %gather_fusion.1), calls=%async_computation | async-start | bytes 1048576 | tf_op jit(solution)/shard_map/all_to_all | solution.py:70
  27.7 2.7 all-to-all-done
  39.5 3.4 fusion.6
  45.9 4.0 %fusion.25 = bf16[128,8,128]{2,0,1:T(8,128)(2,1)} fusion(f32[896,128,8]{1,0,2:T(8,128)} %copy-done.3, f32[8,128]{1,0:T(8,128)S(1)} %get-tuple-element.6, f32[8,128]{1,0:T(8,128)S(1)} %get-tuple-element.30, pred[128,896]{0,1:T(8,128)(4,1)} %concatenate.44, bf16[512,256]{1,0:T(8,128)(2,1)} %get-tuple-element.21, bf16[384,256]{1,0:T(8,128)(2,1)} %copy-done.14), kind=kOutput, calls=%fused_computation.52 | convolution fusion | flops 240058368 | bytes 4513792 | tf_op jit(solution)/shard_map/gtk,kd->tgd/dot_general | solution.py:48
  51.7 4.0 %fusion.24 = bf16[128,8,128]{2,0,1:T(8,128)(2,1)} fusion(f32[896,128,8]{1,0,2:T(8,128)} %copy-done.2, f32[8,128]{1,0:T(8,128)S(1)} %get-tuple-element.7, f32[8,128]{1,0:T(8,128)S(1)} %get-tuple-element.29, pred[128,896]{0,1:T(8,128)(4,1)} %concatenate.44, bf16[384,256]{1,0:T(8,128)(2,1)} %copy-done.14, bf16[512,256]{1,0:T(8,128)(2,1)} %get-tuple-element.21), kind=kOutput, calls=%fused_computation.51 | convolution fusion | flops 240058368 | bytes 4513792 | tf_op jit(solution)/shard_map/gtk,kd->tgd/dot_general | solution.py:48
  57.5 4.0 %fusion.23 = bf16[128,8,128]{2,0,1:T(8,128)(2,1)} fusion(f32[896,128,8]{1,0,2:T(8,128)} %copy-done.1, f32[8,128]{1,0:T(8,128)S(1)} %get-tuple-element.8, f32[8,128]{1,0:T(8,128)S(1)} %get-tuple-element.28, pred[128,896]{0,1:T(8,128)(4,1)} %concatenate.44, bf16[384,256]{1,0:T(8,128)(2,1)} %copy-done.14, bf16[512,256]{1,0:T(8,128)(2,1)} %get-tuple-element.21), kind=kOutput, calls=%fused_computation.50 | convolution fusion | flops 240058368 | bytes 4513792 | tf_op jit(solution)/shard_map/gtk,kd->tgd/dot_general | solution.py:48
  65.1 2.8 multiply_convert_fusion
  67.9 6.6 %gather_fusion.3 = bf16[256,4096]{1,0:T(8,128)(2,1)} fusion(bf16[128,4096]{1,0:T(8,128)(2,1)} %multiply_convert_fusion, s32[1024]{0:T(1024)S(1)} %pad_clamp_fusion), kind=kCustom, calls=%fused_computation.3 | custom fusion | bytes 4195328 | tf_op jit(solution)/shard_map/gather | solution.py:93
  76.5 66.6 %scatter_fusion = bf16[8,48,4096]{2,1,0:T(8,128)(2,1)} fusion(bf16[8,48,4096]{2,1,0:T(8,128)(2,1)} %broadcast_in_dim.33, s32[256]{0:T(256)S(1)} %bitcast.187, bf16[256,4096]{1,0:T(8,128)(2,1)} %gather_fusion.3), kind=kCustom, calls=%fused_computation.6 | custom fusion | bytes 6293504 | tf_op jit(solution)/shard_map/scatter | solution.py:93
  143.1 79.2 %all_to_all.15 = bf16[16,24,4096]{2,1,0:T(8,128)(2,1)} all-to-all(bf16[16,24,4096]{2,1,0:T(8,128)(2,1)} %bitcast.184), channel_id=1, replica_groups=mesh['rollout'=2,'branch'=4,'seq'=4] {'branch','seq'}, dimensions={0} | all-to-all | bytes 6291456 | tf_op jit(solution)/shard_map/all_to_all | solution.py:97
  222.5 5.9 %collective-permute-done = bf16[16,24,4096]{2,1,0:T(8,128)(2,1)} collective-permute-done((bf16[16,24,4096]{2,1,0:T(8,128)(2,1)}, bf16[16,24,4096]{2,1,0:T(8,128)(2,1)}, u32[]{:S(2)}, u32[]{:S(2)}) %collective-permute-start) | collective-permute-done | bytes 3145760 | tf_op jit(solution)/shard_map/ppermute | solution.py:16
  228.4 5.8 %maximum_select_fusion = bf16[16,48,4096]{2,1,0:T(8,128)(2,1)S(1)} fusion(bf16[16,24,4096]{2,1,0:T(8,128)(2,1)} %collective-permute-done, bf16[16,24,4096]{2,1,0:T(8,128)(2,1)} %all_to_all.15, pred[]{:T(512)S(6)} %eq.34), kind=kLoop, calls=%fused_computation.7 | loop fusion | flops 28311552 | bytes 12582913 | tf_op jit(solution)/shard_map/jit(_where)/select_n | solution.py:99
  234.2 7.3 %fusion = f32[768,2,384]{2,0,1:T(8,128)S(1)} fusion(bf16[768,4096,1]{1,0,2:T(8,128)(2,1)S(1)} %bitcast.190, bf16[4096,2,384]{2,1,0:T(2,128)(2,1)} %bitcast.209), kind=kOutput, calls=%fused_computation.8 | convolution fusion | flops 4831838208 | bytes 14942208 | tf_op jit(solution)/shard_map/rd,dcf->rcf/dot_general | solution.py:107
  241.9 4.5 %fusion.18 = f32[16,48,2048]{2,1,0:T(8,128)} fusion(bf16[16,48,384]{2,1,0:T(8,128)(2,1)S(1)} %bitcast.188, bf16[1,384,4096]{2,1,0:T(8,128)(2,1)S(1)} %copy-done, s32[]{:T(128)S(6)} %select_n.199), kind=kOutput, calls=%fused_computation.45 | convolution fusion | flops 1207959552 | bytes 8454148 | tf_op jit(solution)/shard_map/dot_general | solution.py:117
  246.5 10.4 %collective-permute-done.1 = f32[16,48,2048]{2,1,0:T(8,128)} collective-permute-done((f32[16,48,2048]{2,1,0:T(8,128)}, f32[16,48,2048]{2,1,0:T(8,128)}, u32[]{:S(2)}, u32[]{:S(2)}) %collective-permute-start.1) | collective-permute-done | bytes 6291488 | tf_op jit(solution)/shard_map/ppermute | solution.py:16
  256.8 6.5 %add_convert_fusion = bf16[16,48,2048]{2,1,0:T(8,128)(2,1)} fusion(f32[16,48,2048]{2,1,0:T(8,128)} %collective-permute-done.1, bf16[16,48,384]{2,1,0:T(8,128)(2,1)} %bitcast.189, bf16[1,384,4096]{2,1,0:T(8,128)(2,1)S(1)} %copy-done, s32[]{:T(128)S(6)} %select_n.198), kind=kOutput, calls=%fused_computation.10 | convolution fusion | flops 1211105280 | bytes 11599876 | tf_op jit(solution)/shard_map/dot_general | solution.py:114
  263.3 5.3 %all-to-all-start.2 = ((bf16[16,48,2048]{2,1,0:T(8,128)(2,1)}), bf16[16,48,2048]{2,1,0:T(8,128)(2,1)}, u32[]{:S(2)}, u32[]{:S(2)}) async-start(bf16[16,48,2048]{2,1,0:T(8,128)(2,1)} %add_convert_fusion), calls=%async_computation.2 | async-start | bytes 6291456 | tf_op jit(solution)/shard_map/all_to_all | solution.py:122
  278.7 59.8 %all-to-all-done.2 = bf16[16,48,2048]{2,1,0:T(8,128)(2,1)} async-done(((bf16[16,48,2048]{2,1,0:T(8,128)(2,1)}), bf16[16,48,2048]{2,1,0:T(8,128)(2,1)}, u32[]{:S(2)}, u32[]{:S(2)}) %all-to-all-start.2) | async-done | bytes 3145760 | tf_op jit(solution)/shard_map/all_to_all | solution.py:122
  338.5 4.0 %copy.114 = bf16[8,2,6,8,2048]{4,3,1,2,0:T(8,128)(2,1)} copy(bf16[8,2,6,8,2048]{4,3,2,1,0:T(8,128)(2,1)} %bitcast.75) | data formatting | bytes 6291456 | tf_op jit(solution)/shard_map/reshape | solution.py:123
  342.5 7.5 %gather_fusion.4 = bf16[256,4096]{1,0:T(8,128)(2,1)} fusion(bf16[8,48,4096]{2,1,0:T(8,128)(2,1)} %bitcast.185, s32[256]{0:T(256)S(1)} %bitcast.186), kind=kCustom, calls=%fused_computation.4 | custom fusion | bytes 4196352 | tf_op jit(solution)/shard_map/gather | solution.py:126
  350.0 4.4 %reshape.546 = bf16[128,2,4096]{2,1,0:T(2,128)(2,1)} reshape(bf16[256,4096]{1,0:T(8,128)(2,1)} %gather_fusion.4) | data formatting | bytes 4194304 | tf_op jit(solution)/shard_map/reshape | solution.py:126
  354.4 6.2 %fusion.76 = (bf16[128,1,4096]{2,1,0:T(2,128)(2,1)S(1)}, bf16[128,1,4096]{2,1,0:T(2,128)(2,1)S(1)}) fusion(bf16[128,2,4096]{2,1,0:T(2,128)(2,1)} %reshape.546), kind=kLoop, calls=%fused_computation.149 | loop fusion | bytes 4194304 | tf_op jit(solution)/shard_map/slice | solution.py:129
  360.7 5.2 %fusion.12 = bf16[1,128,4096]{2,1,0:T(8,128)(2,1)} fusion(bf16[1,128,4096]{2,1,0:T(8,128)(2,1)S(1)} %copy-done.4, bf16[1,128,1024]{2,1,0:T(8,128)(2,1)S(1)} %copy-done.9, bf16[1,128,1024]{2,1,0:T(8,128)(2,1)S(1)} %copy-done.8, bf16[1,128,1024]{2,1,0:T(8,128)(2,1)S(1)} %copy-done.7, bf16[1,128,1024]{2,1,0:T(8,128)(2,1)S(1)} %copy.77, ...), kind=kLoop, calls=%fused_computation.35 | loop fusion | flops 8912896 | bytes 5243904 | tf_op jit(solution)/shard_map/convert_element_type | solution.py:132
  (98 shorter events, 46.9 us)
Async XLA Ops:
  0.0 241.9 %copy-start = (bf16[1,384,4096]{2,1,0:T(8,128)(2,1)S(1)}, bf16[1,384,4096]{2,1,0:T(8,128)(2,1)}, u32[]{:S(2)}) copy-start(bf16[1,384,4096]{2,1,0:T(8,128)(2,1)} %param.15) | copy-start | bytes 9437188
  0.0 19.1 %copy-start.16 = (s32[1,128,2]{1,2,0:T(2,128)S(1)}, s32[1,128,2]{1,2,0:T(2,128)}, u32[]{:S(2)}) copy-start(s32[1,128,2]{1,2,0:T(2,128)} %param.13) | copy-start | bytes 3076
  14.4 16.0 %all-to-all-start = ((bf16[4,128,2,256]{3,1,2,0:T(8,128)(2,1)}), bf16[4,128,2,256]{3,1,2,0:T(8,128)(2,1)}, u32[]{:S(2)}, u32[]{:S(2)}) async-start(bf16[4,128,2,256]{3,1,2,0:T(8,128)(2,1)} %gather_fusion.1), calls=%async_computation | async-start | bytes 1048576 | tf_op jit(solution)/shard_map/all_to_all | solution.py:70
  32.8 2.8 copy-start.11
  33.9 9.1 %copy-start.14 = (bf16[384,256]{1,0:T(8,128)(2,1)}, bf16[384,256]{1,0:T(8,128)(2,1)S(1)}, u32[]{:S(2)}) copy-start(bf16[384,256]{1,0:T(8,128)(2,1)S(1)} %get-tuple-element.23) | copy-start | bytes 589828
  33.9 2.4 copy-start.10
  35.5 2.9 copy-start.2
  35.6 1.3 copy-start.6
  35.6 1.3 copy-start.12
  36.2 2.3 copy-start.3
  36.9 2.7 copy-start.1
  39.5 3.4 copy-start.13
  222.4 6.0 %collective-permute-start = (bf16[16,24,4096]{2,1,0:T(8,128)(2,1)}, bf16[16,24,4096]{2,1,0:T(8,128)(2,1)}, u32[]{:S(2)}, u32[]{:S(2)}) collective-permute-start(bf16[16,24,4096]{2,1,0:T(8,128)(2,1)} %all_to_all.15), channel_id=1, source_target_pairs={{0,1},{1,0},{2,3},{3,2},{4,5},{5,4},{6,7},{7,6},{8,9},{9,8},{10,11... | collective-permute-start | bytes 9437192 | tf_op jit(solution)/shard_map/ppermute | solution.py:16
  241.9 4.5 %copy-start.5 = (bf16[768,1,384]{2,0,1:T(8,128)(2,1)}, bf16[768,1,384]{2,0,1:T(8,128)(2,1)S(1)}, u32[]{:S(2)}) copy-start(bf16[768,1,384]{2,0,1:T(8,128)(2,1)S(1)} %fusion.27) | copy-start | bytes 1769476
  246.3 10.5 %collective-permute-start.1 = (f32[16,48,2048]{2,1,0:T(8,128)}, f32[16,48,2048]{2,1,0:T(8,128)}, u32[]{:S(2)}, u32[]{:S(2)}) collective-permute-start(f32[16,48,2048]{2,1,0:T(8,128)} %fusion.18), channel_id=1, source_target_pairs={{0,1},{1,0},{2,3},{3,2},{4,5},{5,4},{6,7},{7,6},{8,9},{9,8},{10,11... | collective-permute-start | bytes 18874376 | tf_op jit(solution)/shard_map/ppermute | solution.py:16
  263.3 5.6 %copy-start.15 = (bf16[4096,8]{0,1:T(8,128)(2,1)S(1)}, bf16[4096,8]{0,1:T(8,128)(2,1)}, u32[]{:S(2)}) copy-start(bf16[4096,8]{0,1:T(8,128)(2,1)} %param.12) | copy-start | bytes 196612
  263.3 75.2 %all-to-all-start.2 = ((bf16[16,48,2048]{2,1,0:T(8,128)(2,1)}), bf16[16,48,2048]{2,1,0:T(8,128)(2,1)}, u32[]{:S(2)}, u32[]{:S(2)}) async-start(bf16[16,48,2048]{2,1,0:T(8,128)(2,1)} %add_convert_fusion), calls=%async_computation.2 | async-start | bytes 6291456 | tf_op jit(solution)/shard_map/all_to_all | solution.py:122
  354.4 6.3 %copy-start.4 = (bf16[1,128,4096]{2,1,0:T(8,128)(2,1)S(1)}, bf16[1,128,4096]{2,1,0:T(8,128)(2,1)}, u32[]{:S(2)}) copy-start(bf16[1,128,4096]{2,1,0:T(8,128)(2,1)} %param.10) | copy-start | bytes 3145732
  354.4 6.3 %copy-start.7 = (bf16[1,128,1024]{2,1,0:T(8,128)(2,1)S(1)}, bf16[1,128,1024]{2,1,0:T(8,128)(2,1)}, u32[]{:S(2)}) copy-start(bf16[1,128,1024]{2,1,0:T(8,128)(2,1)} %copy.78) | copy-start | bytes 786436
  354.4 6.3 %copy-start.8 = (bf16[1,128,1024]{2,1,0:T(8,128)(2,1)S(1)}, bf16[1,128,1024]{2,1,0:T(8,128)(2,1)}, u32[]{:S(2)}) copy-start(bf16[1,128,1024]{2,1,0:T(8,128)(2,1)} %copy.79) | copy-start | bytes 786436
  354.4 6.3 %copy-start.9 = (bf16[1,128,1024]{2,1,0:T(8,128)(2,1)S(1)}, bf16[1,128,1024]{2,1,0:T(8,128)(2,1)}, u32[]{:S(2)}) copy-start(bf16[1,128,1024]{2,1,0:T(8,128)(2,1)} %copy.80) | copy-start | bytes 786436
where the time goes:
time: 373 us; the launch traced here: 366 us
  local copies, waits for them, and re-layouts  130 us (35%)
  blocking collectives  87 us (23%)
  waiting for transfers between devices  78.8 us (21%)
  matrix products  38.1 us (10%)
  other arithmetic  21 us (6%)
  starting transfers between devices  10.3 us (3%)
    all_to_all x1, blocking collectives, on_device(): lax.all_to_all(halved, ('branch', 'seq'), split_axis=0, concat_axis=0, ti...  79.2 us
    scatter x1, local copies, waits for them, and re-layouts, on_device(): jnp.zeros((experts, capacity, D), jnp.bfloat16).at[flat_ids, slot_of]  66.6 us
    all_to_all x1, waiting for transfers between devices, on_device(): lax.all_to_all(finished, ('branch', 'seq'), split_axis=0, concat_axis=0,...  59.8 us
    ppermute x2, waiting for transfers between devices, swapped(): return lax.ppermute(value, axis, pairs)  16.3 us
    dot_general x4, matrix products, attend_block(): jnp.einsum('gtk,kd->tgd', probs, value_head, preferred_element_type=jnp.f...  13.8 us
    all_gather x1, blocking collectives, on_device(): suffix_all = lax.all_gather(keyvals, 'seq', axis=1, tiled=True)[0]  7.73 us
    gather x1, local copies, waits for them, and re-layouts, on_device(): expert_out = out_table[flat_ids, slot_of].reshape(block_len, top_count, D)  7.47 us
  transfers between devices with their start and end apart: 4, of which 4 were waited for; matrix products, arithmetic and copies ran while one was open for 5% of the time, Pallas kernels for 0%

commit v1 on v0

--- a/solution.py
+++ b/solution.py
@@ -94,7 +94,19 @@
     )
     pair_half = me_block % 2
     halved = sendbuf.reshape(experts * 2, half_cap, D)
-    own_share = lax.all_to_all(halved, ("branch", "seq"), split_axis=0, concat_axis=0, tiled=True)
+    ways, here = (lax.axis_size(("branch", "seq")), lax.axis_index(("branch", "seq")))
+    width = halved.shape[0] // ways
+    lengths = list(halved.shape)
+    lengths[0] = width
+    height = lengths[0]
+    lengths[0] = height * ways
+    full = jnp.zeros(lengths, halved.dtype)
+    for mask_2 in range(ways):
+        part = lax.dynamic_slice_in_dim(halved, (here ^ mask_2) * width, width, axis=0)
+        if mask_2:
+            part = lax.ppermute(part, ("branch", "seq"), [(d, d ^ mask_2) for d in range(ways)])
+        full = lax.dynamic_update_slice_in_dim(full, part, (here ^ mask_2) * height, axis=0)
+    own_share = full
     theirs = swapped(own_share, "seq", 0)
     rows_in = jnp.where(
         pair_half == 0,

time: 373 us -> 384 us (1.029)
  blocking collectives: 87 us -> 7.73 us
  starting transfers between devices: 10.3 us -> 55.2 us
  waiting for transfers between devices: 78.8 us -> 109 us
  local copies, waits for them, and re-layouts: 130 us -> 145 us
    all_to_all x1 -> x0, blocking collectives: 79.2 us -> none  [on_device(): lax.all_to_all(halved, ('branch', 'seq'), split_axis=0, concat_axis=0, ti...]
    ppermute x0 -> x15, starting transfers between devices: none -> 44.5 us  [on_device(): lax.ppermute(part, ('branch', 'seq'), [(d, d ^ mask_2) for d in range(way...]
    ppermute x0 -> x15, waiting for transfers between devices: none -> 31.2 us  [on_device(): lax.ppermute(part, ('branch', 'seq'), [(d, d ^ mask_2) for d in range(way...]
    dynamic_update_slice x0 -> x15, local copies, waits for them, and re-layouts: none -> 10.4 us  [on_device(): lax.dynamic_update_slice_in_dim(full, part, (here ^ mask_2) * height, axi...]
  transfers between devices with their start and end apart: 4 -> 19, of which waited for: 4 -> 11; matrix products, arithmetic and copies ran while one was open for 5% -> 7% of each run, Pallas kernels for 0% -> 0%
where the time goes in v1:
time: 384 us; the launch traced here: 378 us
  local copies, waits for them, and re-layouts  145 us (38%)
  waiting for transfers between devices  109 us (28%)
  starting transfers between devices  55.2 us (14%)
  matrix products  38.1 us (10%)
  other arithmetic  21 us (5%)
  blocking collectives  7.73 us (2%)
    scatter x1, local copies, waits for them, and re-layouts, on_device(): jnp.zeros((experts, capacity, D), jnp.bfloat16).at[flat_ids, slot_of]  67.4 us
    all_to_all x1, waiting for transfers between devices, on_device(): lax.all_to_all(finished, ('branch', 'seq'), split_axis=0, concat_axis=0,...  59.8 us
    ppermute x15, starting transfers between devices, on_device(): lax.ppermute(part, ('branch', 'seq'), [(d, d ^ mask_2) for d in range(way...  44.5 us
    ppermute x15, waiting for transfers between devices, on_device(): lax.ppermute(part, ('branch', 'seq'), [(d, d ^ mask_2) for d in range(way...  31.2 us
    ppermute x2, waiting for transfers between devices, swapped(): return lax.ppermute(value, axis, pairs)  15.8 us
    dot_general x4, matrix products, attend_block(): jnp.einsum('gtk,kd->tgd', probs, value_head, preferred_element_type=jnp.f...  13.9 us
    dynamic_update_slice x15, local copies, waits for them, and re-layouts, on_device(): lax.dynamic_update_slice_in_dim(full, part, (here ^ mask_2) * height, axi...  10.4 us
    all_gather x1, blocking collectives, on_device(): suffix_all = lax.all_gather(keyvals, 'seq', axis=1, tiled=True)[0]  7.73 us
  transfers between devices with their start and end apart: 19, of which 11 were waited for; matrix products, arithmetic and copies ran while one was open for 7% of the time, Pallas kernels for 0%

profile of v1, /device:TPU:11, one launch (start us, length us, event | category | flops | bytes accessed | tf_op | source)
XLA Modules:
  0.0 377.6 jit_solution(5710029859823294218)
XLA Ops:
  1.1 7.7 %all_gather.3 = bf16[1,512,2,256]{3,1,2,0:T(8,128)(2,1)} all-gather(bf16[1,128,2,256]{3,1,2,0:T(8,128)(2,1)S(1)} %copy.62), channel_id=1, replica_groups=mesh['rollout'=2,'branch'=4,'seq'=4] {'seq'}, dimensions={1}, use_global_device_ids=true | all-gather | bytes 655360 | tf_op jit(solution)/shard_map/all_gather | solution.py:62
  14.4 4.8 %all-to-all-start = ((bf16[4,128,2,256]{3,1,2,0:T(8,128)(2,1)}), bf16[4,128,2,256]{3,1,2,0:T(8,128)(2,1)}, u32[]{:S(2)}, u32[]{:S(2)}) async-start(bf16[4,128,2,256]{3,1,2,0:T(8,128)(2,1)} %gather_fusion.1), calls=%async_computation | async-start | bytes 1048576 | tf_op jit(solution)/shard_map/all_to_all | solution.py:70
  45.8 4.0 %fusion.25 = bf16[128,8,128]{2,0,1:T(8,128)(2,1)} fusion(f32[896,128,8]{1,0,2:T(8,128)} %copy-done.4, f32[8,128]{1,0:T(8,128)S(1)} %get-tuple-element.6, f32[8,128]{1,0:T(8,128)S(1)} %get-tuple-element.47, pred[128,896]{0,1:T(8,128)(4,1)} %concatenate.44, bf16[512,256]{1,0:T(8,128)(2,1)} %get-tuple-element.37, bf16[384,256]{1,0:T(8,128)(2,1)} %copy-done.15), kind=kOutput, calls=%fused_computation.52 | convolution fusion | flops 240058368 | bytes 4513792 | tf_op jit(solution)/shard_map/gtk,kd->tgd/dot_general | solution.py:48
  51.6 4.0 %fusion.24 = bf16[128,8,128]{2,0,1:T(8,128)(2,1)} fusion(f32[896,128,8]{1,0,2:T(8,128)} %copy-done.3, f32[8,128]{1,0:T(8,128)S(1)} %get-tuple-element.7, f32[8,128]{1,0:T(8,128)S(1)} %get-tuple-element.46, pred[128,896]{0,1:T(8,128)(4,1)} %concatenate.44, bf16[384,256]{1,0:T(8,128)(2,1)} %copy-done.15, bf16[512,256]{1,0:T(8,128)(2,1)} %get-tuple-element.37), kind=kOutput, calls=%fused_computation.51 | convolution fusion | flops 240058368 | bytes 4513792 | tf_op jit(solution)/shard_map/gtk,kd->tgd/dot_general | solution.py:48
  57.4 4.0 %fusion.23 = bf16[128,8,128]{2,0,1:T(8,128)(2,1)} fusion(f32[896,128,8]{1,0,2:T(8,128)} %copy-done.2, f32[8,128]{1,0:T(8,128)S(1)} %get-tuple-element.8, f32[8,128]{1,0:T(8,128)S(1)} %get-tuple-element.45, pred[128,896]{0,1:T(8,128)(4,1)} %concatenate.44, bf16[384,256]{1,0:T(8,128)(2,1)} %copy-done.15, bf16[512,256]{1,0:T(8,128)(2,1)} %get-tuple-element.37), kind=kOutput, calls=%fused_computation.50 | convolution fusion | flops 240058368 | bytes 4513792 | tf_op jit(solution)/shard_map/gtk,kd->tgd/dot_general | solution.py:48
  67.9 6.6 %gather_fusion.3 = bf16[256,4096]{1,0:T(8,128)(2,1)} fusion(bf16[128,4096]{1,0:T(8,128)(2,1)} %multiply_convert_fusion, s32[1024]{0:T(1024)S(1)} %pad_clamp_fusion), kind=kCustom, calls=%fused_computation.3 | custom fusion | bytes 4195328 | tf_op jit(solution)/shard_map/gather | solution.py:93
  76.5 67.4 %scatter_fusion = bf16[8,48,4096]{2,1,0:T(8,128)(2,1)} fusion(bf16[8,48,4096]{2,1,0:T(8,128)(2,1)} %broadcast_in_dim.36, s32[256]{0:T(256)S(1)} %bitcast.187, bf16[256,4096]{1,0:T(8,128)(2,1)} %gather_fusion.3), kind=kCustom, calls=%fused_computation.6 | custom fusion | bytes 6293504 | tf_op jit(solution)/shard_map/scatter | solution.py:93
  172.4 6.4 %collective-permute-start.10 = (bf16[1,24,4096]{2,1,0:T(8,128)(2,1)S(1)}, bf16[1,24,4096]{2,1,0:T(8,128)(2,1)S(1)}, u32[]{:S(2)}, u32[]{:S(2)}) collective-permute-start(bf16[1,24,4096]{2,1,0:T(8,128)(2,1)S(1)} %get-tuple-element.19), channel_id=1, source_target_pairs={{0,11},{1,10},{2,9},{3,8},{4,15},{5,14},{6,13},{7,12},{8,3},{9,2},... | collective-permute-start | bytes 589832 | tf_op jit(solution)/shard_map/ppermute | solution.py:107
  181.2 17.7 %collective-permute-start.13 = (bf16[1,24,4096]{2,1,0:T(8,128)(2,1)S(1)}, bf16[1,24,4096]{2,1,0:T(8,128)(2,1)S(1)}, u32[]{:S(2)}, u32[]{:S(2)}) collective-permute-start(bf16[1,24,4096]{2,1,0:T(8,128)(2,1)S(1)} %get-tuple-element.16), channel_id=1, source_target_pairs={{0,14},{1,15},{2,12},{3,13},{4,10},{5,11},{6,8},{7,9},{8,6},{9,7},... | collective-permute-start | bytes 589832 | tf_op jit(solution)/shard_map/ppermute | solution.py:107
  204.5 9.4 %collective-permute-done.10 = bf16[1,24,4096]{2,1,0:T(8,128)(2,1)S(1)} collective-permute-done((bf16[1,24,4096]{2,1,0:T(8,128)(2,1)S(1)}, bf16[1,24,4096]{2,1,0:T(8,128)(2,1)S(1)}, u32[]{:S(2)}, u32[]{:S(2)}) %collective-permute-start.10) | collective-permute-done | bytes 196640 | tf_op jit(solution)/shard_map/ppermute | solution.py:107
  214.6 6.1 %collective-permute-done.11 = bf16[1,24,4096]{2,1,0:T(8,128)(2,1)S(1)} collective-permute-done((bf16[1,24,4096]{2,1,0:T(8,128)(2,1)S(1)}, bf16[1,24,4096]{2,1,0:T(8,128)(2,1)S(1)}, u32[]{:S(2)}, u32[]{:S(2)}) %collective-permute-start.11) | collective-permute-done | bytes 196640 | tf_op jit(solution)/shard_map/ppermute | solution.py:107
  221.5 4.3 %collective-permute-done.12 = bf16[1,24,4096]{2,1,0:T(8,128)(2,1)S(1)} collective-permute-done((bf16[1,24,4096]{2,1,0:T(8,128)(2,1)S(1)}, bf16[1,24,4096]{2,1,0:T(8,128)(2,1)S(1)}, u32[]{:S(2)}, u32[]{:S(2)}) %collective-permute-start.12) | collective-permute-done | bytes 196640 | tf_op jit(solution)/shard_map/ppermute | solution.py:107
  234.4 5.6 %collective-permute-done.15 = bf16[16,24,4096]{2,1,0:T(8,128)(2,1)} collective-permute-done((bf16[16,24,4096]{2,1,0:T(8,128)(2,1)}, bf16[16,24,4096]{2,1,0:T(8,128)(2,1)}, u32[]{:S(2)}, u32[]{:S(2)}) %collective-permute-start.15) | collective-permute-done | bytes 3145760 | tf_op jit(solution)/shard_map/ppermute | solution.py:16
  240.0 5.9 %maximum_select_fusion = bf16[16,48,4096]{2,1,0:T(8,128)(2,1)S(1)} fusion(bf16[16,24,4096]{2,1,0:T(8,128)(2,1)} %collective-permute-done.15, bf16[16,24,4096]{2,1,0:T(8,128)(2,1)} %constant_dynamic-update-slice_fusion, pred[]{:T(512)S(6)} %eq.34), kind=kLoop, calls=%fused_computation.7 | loop fusion | flops 28311552 | bytes 12582913 | tf_op jit(solution)/shard_map/jit(_where)/select_n | solution.py:111
  245.9 7.3 %fusion = f32[768,2,384]{2,0,1:T(8,128)S(1)} fusion(bf16[768,4096,1]{1,0,2:T(8,128)(2,1)S(1)} %bitcast.190, bf16[4096,2,384]{2,1,0:T(2,128)(2,1)} %bitcast.209), kind=kOutput, calls=%fused_computation.8 | convolution fusion | flops 4831838208 | bytes 14942208 | tf_op jit(solution)/shard_map/rd,dcf->rcf/dot_general | solution.py:119
  253.6 4.5 %fusion.18 = f32[16,48,2048]{2,1,0:T(8,128)} fusion(bf16[16,48,384]{2,1,0:T(8,128)(2,1)S(1)} %bitcast.188, bf16[1,384,4096]{2,1,0:T(8,128)(2,1)S(1)} %copy-done, s32[]{:T(128)S(6)} %select_n.279), kind=kOutput, calls=%fused_computation.45 | convolution fusion | flops 1207959552 | bytes 8454148 | tf_op jit(solution)/shard_map/dot_general | solution.py:129
  258.4 10.1 %collective-permute-done.16 = f32[16,48,2048]{2,1,0:T(8,128)} collective-permute-done((f32[16,48,2048]{2,1,0:T(8,128)}, f32[16,48,2048]{2,1,0:T(8,128)}, u32[]{:S(2)}, u32[]{:S(2)}) %collective-permute-start.16) | collective-permute-done | bytes 6291488 | tf_op jit(solution)/shard_map/ppermute | solution.py:16
  268.5 6.5 %add_convert_fusion = bf16[16,48,2048]{2,1,0:T(8,128)(2,1)} fusion(f32[16,48,2048]{2,1,0:T(8,128)} %collective-permute-done.16, bf16[16,48,384]{2,1,0:T(8,128)(2,1)} %bitcast.189, bf16[1,384,4096]{2,1,0:T(8,128)(2,1)S(1)} %copy-done, s32[]{:T(128)S(6)} %select_n.278), kind=kOutput, calls=%fused_computation.10 | convolution fusion | flops 1211105280 | bytes 11599876 | tf_op jit(solution)/shard_map/dot_general | solution.py:126
  275.0 5.2 %all-to-all-start.1 = ((bf16[16,48,2048]{2,1,0:T(8,128)(2,1)}), bf16[16,48,2048]{2,1,0:T(8,128)(2,1)}, u32[]{:S(2)}, u32[]{:S(2)}) async-start(bf16[16,48,2048]{2,1,0:T(8,128)(2,1)} %add_convert_fusion), calls=%async_computation.1 | async-start | bytes 6291456 | tf_op jit(solution)/shard_map/all_to_all | solution.py:134
  290.2 59.8 %all-to-all-done.1 = bf16[16,48,2048]{2,1,0:T(8,128)(2,1)} async-done(((bf16[16,48,2048]{2,1,0:T(8,128)(2,1)}), bf16[16,48,2048]{2,1,0:T(8,128)(2,1)}, u32[]{:S(2)}, u32[]{:S(2)}) %all-to-all-start.1) | async-done | bytes 3145760 | tf_op jit(solution)/shard_map/all_to_all | solution.py:134
  354.0 7.5 %gather_fusion.4 = bf16[256,4096]{1,0:T(8,128)(2,1)} fusion(bf16[8,48,4096]{2,1,0:T(8,128)(2,1)} %bitcast.185, s32[256]{0:T(256)S(1)} %bitcast.186), kind=kCustom, calls=%fused_computation.4 | custom fusion | bytes 4196352 | tf_op jit(solution)/shard_map/gather | solution.py:138
  361.5 4.4 %reshape.546 = bf16[128,2,4096]{2,1,0:T(2,128)(2,1)} reshape(bf16[256,4096]{1,0:T(8,128)(2,1)} %gather_fusion.4) | data formatting | bytes 4194304 | tf_op jit(solution)/shard_map/reshape | solution.py:138
  365.9 6.1 %fusion.76 = (bf16[128,1,4096]{2,1,0:T(2,128)(2,1)S(1)}, bf16[128,1,4096]{2,1,0:T(2,128)(2,1)S(1)}) fusion(bf16[128,2,4096]{2,1,0:T(2,128)(2,1)} %reshape.546), kind=kLoop, calls=%fused_computation.180 | loop fusion | bytes 4194304 | tf_op jit(solution)/shard_map/slice | solution.py:141
  372.1 5.2 %fusion.12 = bf16[1,128,4096]{2,1,0:T(8,128)(2,1)} fusion(bf16[1,128,4096]{2,1,0:T(8,128)(2,1)S(1)} %copy-done.5, bf16[1,128,1024]{2,1,0:T(8,128)(2,1)S(1)} %copy-done.10, bf16[1,128,1024]{2,1,0:T(8,128)(2,1)S(1)} %copy-done.9, bf16[1,128,1024]{2,1,0:T(8,128)(2,1)S(1)} %copy-done.8, bf16[1,128,1024]{2,1,0:T(8,128)(2,1)S(1)} %copy.77, ...), kind=kLoop, calls=%fused_computation.35 | loop fusion | flops 8912896 | bytes 5243904 | tf_op jit(solution)/shard_map/convert_element_type | solution.py:144
  (145 shorter events, 106.3 us)
Async XLA Ops:
  0.0 253.6 %copy-start = (bf16[1,384,4096]{2,1,0:T(8,128)(2,1)S(1)}, bf16[1,384,4096]{2,1,0:T(8,128)(2,1)}, u32[]{:S(2)}) copy-start(bf16[1,384,4096]{2,1,0:T(8,128)(2,1)} %param.15) | copy-start | bytes 9437188
  0.0 19.1 %copy-start.17 = (s32[1,128,2]{1,2,0:T(2,128)S(1)}, s32[1,128,2]{1,2,0:T(2,128)}, u32[]{:S(2)}) copy-start(s32[1,128,2]{1,2,0:T(2,128)} %param.13) | copy-start | bytes 3076
  14.4 16.0 %all-to-all-start = ((bf16[4,128,2,256]{3,1,2,0:T(8,128)(2,1)}), bf16[4,128,2,256]{3,1,2,0:T(8,128)(2,1)}, u32[]{:S(2)}, u32[]{:S(2)}) async-start(bf16[4,128,2,256]{3,1,2,0:T(8,128)(2,1)} %gather_fusion.1), calls=%async_computation | async-start | bytes 1048576 | tf_op jit(solution)/shard_map/all_to_all | solution.py:70
  33.8 9.1 %copy-start.15 = (bf16[384,256]{1,0:T(8,128)(2,1)}, bf16[384,256]{1,0:T(8,128)(2,1)S(1)}, u32[]{:S(2)}) copy-start(bf16[384,256]{1,0:T(8,128)(2,1)S(1)} %get-tuple-element.39) | copy-start | bytes 589828
  147.9 6.6 %collective-permute-start = (bf16[1,24,4096]{2,1,0:T(8,128)(2,1)S(1)}, bf16[1,24,4096]{2,1,0:T(8,128)(2,1)S(1)}, u32[]{:S(2)}, u32[]{:S(2)}) collective-permute-start(bf16[1,24,4096]{2,1,0:T(8,128)(2,1)S(1)} %get-tuple-element.29), channel_id=1, source_target_pairs={{0,1},{1,0},{2,3},{3,2},{4,5},{5,4},{6,7},{7,6},{8,9},{9,8},{10,11... | collective-permute-start | bytes 589832 | tf_op jit(solution)/shard_map/ppermute | solution.py:107
  149.8 6.9 %collective-permute-start.1 = (bf16[1,24,4096]{2,1,0:T(8,128)(2,1)S(1)}, bf16[1,24,4096]{2,1,0:T(8,128)(2,1)S(1)}, u32[]{:S(2)}, u32[]{:S(2)}) collective-permute-start(bf16[1,24,4096]{2,1,0:T(8,128)(2,1)S(1)} %get-tuple-element.28), channel_id=1, source_target_pairs={{0,2},{1,3},{2,0},{3,1},{4,6},{5,7},{6,4},{7,5},{8,10},{9,11},{10,... | collective-permute-start | bytes 589832 | tf_op jit(solution)/shard_map/ppermute | solution.py:107
  150.2 10.8 %collective-permute-start.2 = (bf16[1,24,4096]{2,1,0:T(8,128)(2,1)S(1)}, bf16[1,24,4096]{2,1,0:T(8,128)(2,1)S(1)}, u32[]{:S(2)}, u32[]{:S(2)}) collective-permute-start(bf16[1,24,4096]{2,1,0:T(8,128)(2,1)S(1)} %get-tuple-element.27), channel_id=1, source_target_pairs={{0,3},{1,2},{2,1},{3,0},{4,7},{5,6},{6,5},{7,4},{8,11},{9,10},{10,... | collective-permute-start | bytes 589832 | tf_op jit(solution)/shard_map/ppermute | solution.py:107
  151.4 12.5 %collective-permute-start.3 = (bf16[1,24,4096]{2,1,0:T(8,128)(2,1)S(1)}, bf16[1,24,4096]{2,1,0:T(8,128)(2,1)S(1)}, u32[]{:S(2)}, u32[]{:S(2)}) collective-permute-start(bf16[1,24,4096]{2,1,0:T(8,128)(2,1)S(1)} %get-tuple-element.26), channel_id=1, source_target_pairs={{0,4},{1,5},{2,6},{3,7},{4,0},{5,1},{6,2},{7,3},{8,12},{9,13},{10,... | collective-permute-start | bytes 589832 | tf_op jit(solution)/shard_map/ppermute | solution.py:107
  154.4 10.4 %collective-permute-start.4 = (bf16[1,24,4096]{2,1,0:T(8,128)(2,1)S(1)}, bf16[1,24,4096]{2,1,0:T(8,128)(2,1)S(1)}, u32[]{:S(2)}, u32[]{:S(2)}) collective-permute-start(bf16[1,24,4096]{2,1,0:T(8,128)(2,1)S(1)} %get-tuple-element.25), channel_id=1, source_target_pairs={{0,5},{1,4},{2,7},{3,6},{4,1},{5,0},{6,3},{7,2},{8,13},{9,12},{10,... | collective-permute-start | bytes 589832 | tf_op jit(solution)/shard_map/ppermute | solution.py:107
  154.5 17.9 %collective-permute-start.5 = (bf16[1,24,4096]{2,1,0:T(8,128)(2,1)S(1)}, bf16[1,24,4096]{2,1,0:T(8,128)(2,1)S(1)}, u32[]{:S(2)}, u32[]{:S(2)}) collective-permute-start(bf16[1,24,4096]{2,1,0:T(8,128)(2,1)S(1)} %get-tuple-element.24), channel_id=1, source_target_pairs={{0,6},{1,7},{2,4},{3,5},{4,2},{5,3},{6,0},{7,1},{8,14},{9,15},{10,... | collective-permute-start | bytes 589832 | tf_op jit(solution)/shard_map/ppermute | solution.py:107
  156.7 22.8 %collective-permute-start.6 = (bf16[1,24,4096]{2,1,0:T(8,128)(2,1)S(1)}, bf16[1,24,4096]{2,1,0:T(8,128)(2,1)S(1)}, u32[]{:S(2)}, u32[]{:S(2)}) collective-permute-start(bf16[1,24,4096]{2,1,0:T(8,128)(2,1)S(1)} %get-tuple-element.23), channel_id=1, source_target_pairs={{0,7},{1,6},{2,5},{3,4},{4,3},{5,2},{6,1},{7,0},{8,15},{9,14},{10,... | collective-permute-start | bytes 589832 | tf_op jit(solution)/shard_map/ppermute | solution.py:107
  161.0 19.1 %collective-permute-start.7 = (bf16[1,24,4096]{2,1,0:T(8,128)(2,1)S(1)}, bf16[1,24,4096]{2,1,0:T(8,128)(2,1)S(1)}, u32[]{:S(2)}, u32[]{:S(2)}) collective-permute-start(bf16[1,24,4096]{2,1,0:T(8,128)(2,1)S(1)} %get-tuple-element.22), channel_id=1, source_target_pairs={{0,8},{1,9},{2,10},{3,11},{4,12},{5,13},{6,14},{7,15},{8,0},{9,1},... | collective-permute-start | bytes 589832 | tf_op jit(solution)/shard_map/ppermute | solution.py:107
  163.9 17.3 %collective-permute-start.8 = (bf16[1,24,4096]{2,1,0:T(8,128)(2,1)S(1)}, bf16[1,24,4096]{2,1,0:T(8,128)(2,1)S(1)}, u32[]{:S(2)}, u32[]{:S(2)}) collective-permute-start(bf16[1,24,4096]{2,1,0:T(8,128)(2,1)S(1)} %get-tuple-element.21), channel_id=1, source_target_pairs={{0,9},{1,8},{2,11},{3,10},{4,13},{5,12},{6,15},{7,14},{8,1},{9,0},... | collective-permute-start | bytes 589832 | tf_op jit(solution)/shard_map/ppermute | solution.py:107
  164.8 36.5 %collective-permute-start.9 = (bf16[1,24,4096]{2,1,0:T(8,128)(2,1)S(1)}, bf16[1,24,4096]{2,1,0:T(8,128)(2,1)S(1)}, u32[]{:S(2)}, u32[]{:S(2)}) collective-permute-start(bf16[1,24,4096]{2,1,0:T(8,128)(2,1)S(1)} %get-tuple-element.20), channel_id=1, source_target_pairs={{0,10},{1,11},{2,8},{3,9},{4,14},{5,15},{6,12},{7,13},{8,2},{9,3},... | collective-permute-start | bytes 589832 | tf_op jit(solution)/shard_map/ppermute | solution.py:107
  172.4 41.5 %collective-permute-start.10 = (bf16[1,24,4096]{2,1,0:T(8,128)(2,1)S(1)}, bf16[1,24,4096]{2,1,0:T(8,128)(2,1)S(1)}, u32[]{:S(2)}, u32[]{:S(2)}) collective-permute-start(bf16[1,24,4096]{2,1,0:T(8,128)(2,1)S(1)} %get-tuple-element.19), channel_id=1, source_target_pairs={{0,11},{1,10},{2,9},{3,8},{4,15},{5,14},{6,13},{7,12},{8,3},{9,2},... | collective-permute-start | bytes 589832 | tf_op jit(solution)/shard_map/ppermute | solution.py:107
  179.5 41.3 %collective-permute-start.11 = (bf16[1,24,4096]{2,1,0:T(8,128)(2,1)S(1)}, bf16[1,24,4096]{2,1,0:T(8,128)(2,1)S(1)}, u32[]{:S(2)}, u32[]{:S(2)}) collective-permute-start(bf16[1,24,4096]{2,1,0:T(8,128)(2,1)S(1)} %get-tuple-element.18), channel_id=1, source_target_pairs={{0,12},{1,13},{2,14},{3,15},{4,8},{5,9},{6,10},{7,11},{8,4},{9,5},... | collective-permute-start | bytes 589832 | tf_op jit(solution)/shard_map/ppermute | solution.py:107
  180.1 45.6 %collective-permute-start.12 = (bf16[1,24,4096]{2,1,0:T(8,128)(2,1)S(1)}, bf16[1,24,4096]{2,1,0:T(8,128)(2,1)S(1)}, u32[]{:S(2)}, u32[]{:S(2)}) collective-permute-start(bf16[1,24,4096]{2,1,0:T(8,128)(2,1)S(1)} %get-tuple-element.17), channel_id=1, source_target_pairs={{0,13},{1,12},{2,15},{3,14},{4,9},{5,8},{6,11},{7,10},{8,5},{9,4},... | collective-permute-start | bytes 589832 | tf_op jit(solution)/shard_map/ppermute | solution.py:107
  181.2 47.9 %collective-permute-start.13 = (bf16[1,24,4096]{2,1,0:T(8,128)(2,1)S(1)}, bf16[1,24,4096]{2,1,0:T(8,128)(2,1)S(1)}, u32[]{:S(2)}, u32[]{:S(2)}) collective-permute-start(bf16[1,24,4096]{2,1,0:T(8,128)(2,1)S(1)} %get-tuple-element.16), channel_id=1, source_target_pairs={{0,14},{1,15},{2,12},{3,13},{4,10},{5,11},{6,8},{7,9},{8,6},{9,7},... | collective-permute-start | bytes 589832 | tf_op jit(solution)/shard_map/ppermute | solution.py:107
  201.3 32.0 %collective-permute-start.14 = (bf16[1,24,4096]{2,1,0:T(8,128)(2,1)S(1)}, bf16[1,24,4096]{2,1,0:T(8,128)(2,1)S(1)}, u32[]{:S(2)}, u32[]{:S(2)}) collective-permute-start(bf16[1,24,4096]{2,1,0:T(8,128)(2,1)S(1)} %get-tuple-element.15), channel_id=1, source_target_pairs={{0,15},{1,14},{2,13},{3,12},{4,11},{5,10},{6,9},{7,8},{8,7},{9,6},... | collective-permute-start | bytes 589832 | tf_op jit(solution)/shard_map/ppermute | solution.py:107
  234.0 6.0 %collective-permute-start.15 = (bf16[16,24,4096]{2,1,0:T(8,128)(2,1)}, bf16[16,24,4096]{2,1,0:T(8,128)(2,1)}, u32[]{:S(2)}, u32[]{:S(2)}) collective-permute-start(bf16[16,24,4096]{2,1,0:T(8,128)(2,1)} %constant_dynamic-update-slice_fusion), channel_id=1, source_target_pairs={{0,1},{1,0},{2,3},{3,2},{4,5},{5,4},{6,7},{7,6},{8,9},{9,8},{10,11... | collective-permute-start | bytes 9437192 | tf_op jit(solution)/shard_map/ppermute | solution.py:16
  258.0 10.5 %collective-permute-start.16 = (f32[16,48,2048]{2,1,0:T(8,128)}, f32[16,48,2048]{2,1,0:T(8,128)}, u32[]{:S(2)}, u32[]{:S(2)}) collective-permute-start(f32[16,48,2048]{2,1,0:T(8,128)} %fusion.18), channel_id=1, source_target_pairs={{0,1},{1,0},{2,3},{3,2},{4,5},{5,4},{6,7},{7,6},{8,9},{9,8},{10,11... | collective-permute-start | bytes 18874376 | tf_op jit(solution)/shard_map/ppermute | solution.py:16
  275.0 75.0 %all-to-all-start.1 = ((bf16[16,48,2048]{2,1,0:T(8,128)(2,1)}), bf16[16,48,2048]{2,1,0:T(8,128)(2,1)}, u32[]{:S(2)}, u32[]{:S(2)}) async-start(bf16[16,48,2048]{2,1,0:T(8,128)(2,1)} %add_convert_fusion), calls=%async_computation.1 | async-start | bytes 6291456 | tf_op jit(solution)/shard_map/all_to_all | solution.py:134
  365.9 6.2 %copy-start.9 = (bf16[1,128,1024]{2,1,0:T(8,128)(2,1)S(1)}, bf16[1,128,1024]{2,1,0:T(8,128)(2,1)}, u32[]{:S(2)}) copy-start(bf16[1,128,1024]{2,1,0:T(8,128)(2,1)} %copy.79) | copy-start | bytes 786436
  365.9 6.2 %copy-start.10 = (bf16[1,128,1024]{2,1,0:T(8,128)(2,1)S(1)}, bf16[1,128,1024]{2,1,0:T(8,128)(2,1)}, u32[]{:S(2)}) copy-start(bf16[1,128,1024]{2,1,0:T(8,128)(2,1)} %copy.80) | copy-start | bytes 786436
  (13 other events, 43.6 us)
